TPU v7x, 32 devices: a whole 2x2x4 slice. The times are simulated.
32 devices in a mesh: row: 4 (over y, core), col: 8 (over z, x).
Axes of the slice: x: 2, y: 2, z: 4, core: 2. Of those that a mesh axis runs over, the one named last changes fastest.
Arguments:
- support_views: float32 [256, 4, 3, 1024], P(('row', 'col')), may hold values from -6 to 6
- support_pick: int32 [256], P(('row', 'col')), may hold values from 0 to 3
- target_views: float32 [256, 4, 3, 1024], P(('row', 'col')), may hold values from -6 to 6
- target_pick: int32 [256], P(('row', 'col')), may hold values from 0 to 3
- support_labels: float32 [256, 10], P(('row', 'col')), may hold values from -6 to 6
- target_labels: int32 [256], replicated, may hold values from 0 to 9
Outputs:
- support_grad: float32 [256, 3, 1024], P(('row', 'col'))
- label_grad: float32 [256, 10], P(('row', 'col'))
- loss: float32 [], replicated
All inputs are finite; a program needn't handle non-finite values.
Results may differ from a plain program's by a relative error of at most 0.00055.
Values sent between devices are 32-bit elements; how exact they have to be, the bound alone decides.
No kernel may reach another device: no remote copies, remote signals or barrier semaphores. Data moves between devices by JAX's collectives and lax.ppermute only.
A program may use at most 64 MiB of HBM per device.

v0:
```python
import math
import jax
import jax.numpy as jnp
from jax import lax
from jax.sharding import PartitionSpec as P

SIDE = 32
LAYERS = 3
SUPPORT = 256
bias_variance = 0.1
ridge_scale = 0.1
highest = lax.Precision.HIGHEST


def shifted(surface, offset):
    extent = surface.shape[-1]
    padding = jnp.zeros(surface.shape[:-1] + (abs(offset),), surface.dtype)
    if offset > 0:
        return jnp.concatenate([surface[..., offset:], padding], axis=-1)
    return jnp.concatenate([padding, surface[..., : extent + offset]], axis=-1)


def average(surface):
    column = jnp.arange(surface.shape[-1], dtype=jnp.int32) % SIDE
    rightward = jnp.where(column < SIDE - 1, shifted(surface, 1), 0.0)
    leftward = jnp.where(column > 0, shifted(surface, -1), 0.0)
    across = surface + leftward + rightward
    return (across + shifted(across, SIDE) + shifted(across, -SIDE)) / 9.0


def choose_view(views, picked):
    options = jnp.arange(views.shape[1], dtype=jnp.int32)
    selector = (picked[:, None] == options[None, :]).astype(jnp.float32)
    return jnp.sum(selector[:, :, None, None] * views, axis=1)


def self_maps(images):
    energy = jnp.sum(images * images, axis=1) / images.shape[1]
    current = average(energy) + bias_variance
    stacked = [current]
    for layer in range(1, LAYERS):
        current = average(current) + bias_variance
        stacked.append(current)
    return jnp.stack(stacked, axis=1)


def self_back(images, grad_maps):
    carry = grad_maps[:, -1]
    for layer in range(grad_maps.shape[1] - 2, -1, -1):
        carry = grad_maps[:, layer] + average(carry)
    return average(carry)[:, None, :] * images * (2.0 / images.shape[1])


def arc(kernel_map, first_diag, second_diag):
    scale_map = jnp.sqrt(first_diag * second_diag)
    cosine = jnp.clip(kernel_map / scale_map, -1.0, 1.0)
    sine = jnp.sqrt(1.0 - cosine * cosine)
    angle = jnp.arccos(cosine)
    value = scale_map * (sine + (jnp.pi - angle) * cosine) / jnp.pi
    slope = (jnp.pi - angle) / jnp.pi
    spread = scale_map * sine / (2.0 * jnp.pi)
    return (value, slope, spread)


def pair_forward(first, first_maps, second, second_maps):
    product = first[:, None, 0] * second[None, :, 0]
    for channel in range(1, first.shape[1]):
        product = product + first[:, None, channel] * second[None, :, channel]
    current = average(product / first.shape[1]) + bias_variance
    slopes = []
    spreads = []
    depth = first_maps.shape[1]
    for layer in range(depth):
        value, slope, spread = arc(current, first_maps[:, None, layer], second_maps[None, :, layer])
        slopes.append(slope)
        spreads.append(spread)
        if layer + 1 < depth:
            current = average(value) + bias_variance
    return (jnp.mean(value, axis=-1), slopes, spreads)


def pair_backward(first, first_maps, second, second_maps, weights, want_second):
    kernel, slopes, spreads = pair_forward(first, first_maps, second, second_maps)
    depth = first_maps.shape[1]
    grad = jnp.broadcast_to(weights[:, :, None] / first.shape[-1], slopes[0].shape)
    first_parts = []
    second_parts = []
    for layer in range(depth - 1, -1, -1):
        scaled = grad * spreads[layer]
        first_parts.insert(0, jnp.sum(scaled, axis=1) / first_maps[:, layer])
        if want_second:
            second_parts.insert(0, jnp.sum(scaled, axis=0) / second_maps[:, layer])
        grad = average(grad * slopes[layer])
    first_image = (
        jnp.stack(
            [jnp.sum(grad * second[None, :, channel], axis=1) for channel in range(first.shape[1])],
            axis=1,
        )
        / first.shape[1]
    )
    if not want_second:
        return (first_image, jnp.stack(first_parts, axis=1), None, None)
    second_image = (
        jnp.stack(
            [jnp.sum(grad * first[:, None, channel], axis=0) for channel in range(first.shape[1])],
            axis=1,
        )
        / first.shape[1]
    )
    return (
        first_image,
        jnp.stack(first_parts, axis=1),
        second_image,
        jnp.stack(second_parts, axis=1),
    )


def blocked_kernel(first, first_maps, second, second_maps):
    block_width = math.gcd(second.shape[0], 4)
    block_count = second.shape[0] // block_width

    def one_block(inputs):
        part_images, part_maps = inputs
        kernel, _, _ = pair_forward(first, first_maps, part_images, part_maps)
        return kernel

    pieces = lax.map(
        one_block,
        (
            second.reshape((block_count, block_width) + second.shape[1:]),
            second_maps.reshape((block_count, block_width) + second_maps.shape[1:]),
        ),
    )
    return jnp.transpose(pieces, (1, 0, 2)).reshape(first.shape[0], second.shape[0])


def blocked_backward(first, first_maps, second, second_maps, weights, want_second):
    block_width = math.gcd(second.shape[0], 4)
    block_count = second.shape[0] // block_width
    block_weights = jnp.transpose(
        weights.reshape(first.shape[0], block_count, block_width), (1, 0, 2)
    )

    def one_block(carry, inputs):
        part_images, part_maps, part_weights = inputs
        grad_first, maps_first, grad_second, maps_second = pair_backward(
            first, first_maps, part_images, part_maps, part_weights, want_second
        )
        return ((carry[0] + grad_first, carry[1] + maps_first), (grad_second, maps_second))

    start = (jnp.zeros(first.shape, jnp.float32), jnp.zeros(first_maps.shape, jnp.float32))
    (first_grad, first_map_grad), (second_grad, second_map_grad) = lax.scan(
        one_block,
        start,
        (
            second.reshape((block_count, block_width) + second.shape[1:]),
            second_maps.reshape((block_count, block_width) + second_maps.shape[1:]),
            block_weights,
        ),
    )
    if not want_second:
        return (first_grad, first_map_grad, None, None)
    return (
        first_grad,
        first_map_grad,
        second_grad.reshape(second.shape),
        second_map_grad.reshape(second_maps.shape),
    )


def solve_with(factor, rhs):
    halfway = lax.linalg.triangular_solve(factor, rhs, left_side=True, lower=True)
    return lax.linalg.triangular_solve(
        factor, halfway, left_side=True, lower=True, transpose_a=True
    )


def assemble_folded(tiles, row_count, col_count, own_count, picks):
    span = col_count * own_count
    shaped = tiles.reshape(row_count, col_count, span, picks, own_count)
    block_ids = jnp.arange(row_count, dtype=jnp.int32)
    offsets = jnp.arange(picks, dtype=jnp.int32)
    selector = (
        block_ids[None, None, :] == (block_ids[:, None, None] + offsets[None, :, None]) % row_count
    ).astype(jnp.float32)
    upper = jnp.einsum("rcadk,rdq->raqck", shaped, selector, precision=highest)
    upper = upper.reshape(row_count * span, row_count * span)
    return upper + upper.T - jnp.diag(jnp.diag(upper))


def column_of(matrix, col_index, row_count, col_count, per_device):
    shaped = matrix.reshape(row_count, col_count, per_device, matrix.shape[-1])
    picked = lax.dynamic_index_in_dim(shaped, col_index, 1, keepdims=False)
    return picked.reshape(row_count * per_device, matrix.shape[-1])


def pick_blocks(stacked, row_index, row_count, own_count, picks):
    shaped = stacked.reshape((row_count, own_count) + stacked.shape[1:])
    rolled = jnp.roll(shaped, -row_index, axis=0)[:picks]
    return rolled.reshape((picks * own_count,) + stacked.shape[1:])


def place_blocks(picked, row_index, row_count, own_count, picks):
    shaped = picked.reshape((picks, own_count) + picked.shape[1:])
    padding = jnp.zeros((row_count - picks, own_count) + picked.shape[1:], picked.dtype)
    full = jnp.roll(jnp.concatenate([shaped, padding], axis=0), row_index, axis=0)
    return full.reshape((row_count * own_count,) + picked.shape[1:])


def body(support_views, support_pick, target_views, target_pick, support_labels, target_labels):
    row_count = lax.axis_size("row")
    col_count = lax.axis_size("col")
    row_index = lax.axis_index("row")
    col_index = lax.axis_index("col")
    own_count = support_views.shape[0]
    own_targets = target_views.shape[0]
    channels = support_views.shape[2]
    classes = support_labels.shape[1]
    own_support = choose_view(support_views, support_pick)
    own_target = choose_view(target_views, target_pick)
    support_pack = jnp.concatenate([own_support, self_maps(own_support)], axis=1)
    target_pack = jnp.concatenate([own_target, self_maps(own_target)], axis=1)
    row_pack = lax.all_gather(support_pack, "col", axis=0, tiled=True)
    column_pack, target_block = (
        lax.all_gather(support_pack, "row", axis=0, tiled=True),
        lax.all_gather(target_pack, "row", axis=0, tiled=True),
    )
    row_images = row_pack[:, :channels]
    row_maps = row_pack[:, channels:]
    column_images = column_pack[:, :channels]
    column_maps = column_pack[:, channels:]
    target_images = target_block[:, :channels]
    target_maps = target_block[:, channels:]
    row_start = row_index * col_count * own_count
    row_span = col_count * own_count
    half_count = row_count // 2
    picks = half_count + 1
    chosen_images = pick_blocks(column_images, row_index, row_count, own_count, picks)
    chosen_maps = pick_blocks(column_maps, row_index, row_count, own_count, picks)
    slot_ids = jnp.arange(picks * own_count, dtype=jnp.int32)
    offset_ids = slot_ids // own_count
    inner_ids = slot_ids % own_count
    local_cols = col_index * own_count + inner_ids
    chosen_global = (
        (row_index + offset_ids) % row_count * col_count + col_index
    ) * own_count + inner_ids
    row_ids = jnp.arange(row_span, dtype=jnp.int32)
    keep = jnp.where(
        offset_ids[None, :] == 0,
        row_ids[:, None] <= local_cols[None, :],
        jnp.where(offset_ids[None, :] == half_count, row_index < half_count, True),
    )
    keep_mask = keep.astype(jnp.float32)
    equal_mask = ((offset_ids[None, :] == 0) & (row_ids[:, None] == local_cols[None, :])).astype(
        jnp.float32
    )
    support_tile = blocked_kernel(row_images, row_maps, chosen_images, chosen_maps) * keep_mask
    cross_tile = blocked_kernel(row_images, row_maps, target_images, target_maps)
    onehot_all = (target_labels[:, None] == jnp.arange(classes, dtype=jnp.int32)[None, :]).astype(
        jnp.float32
    ) - 1.0 / classes
    identity = jnp.eye(SUPPORT, dtype=jnp.float32)
    tiles, all_labels = (
        lax.all_gather(support_tile, ("row", "col"), axis=0, tiled=True),
        lax.all_gather(support_labels, ("row", "col"), axis=0, tiled=True),
    )
    support_kernel = assemble_folded(tiles, row_count, col_count, own_count, picks)
    trace_mean = jnp.trace(support_kernel) / SUPPORT
    factor = jnp.linalg.cholesky(support_kernel + ridge_scale * trace_mean * identity)
    alpha = solve_with(factor, all_labels)
    alpha_rows = lax.dynamic_slice_in_dim(alpha, row_start, row_span, 0)
    labels_here = column_of(onehot_all, col_index, row_count, col_count, own_targets)
    predicted = lax.psum(jnp.dot(cross_tile.T, alpha_rows, precision=highest), "row")
    error = predicted - labels_here
    adjoint_part, loss_sum = lax.psum(
        (jnp.dot(cross_tile, error, precision=highest), jnp.sum(error * error)), "col"
    )
    adjoint = lax.all_gather(adjoint_part, "row", axis=0, tiled=True)
    gamma = solve_with(factor, adjoint)
    intersection = jnp.sum(gamma * alpha)
    gamma_rows = lax.dynamic_slice_in_dim(gamma, row_start, row_span, 0)
    cross_weights = jnp.dot(alpha_rows, error.T, precision=highest)
    alpha_chosen = alpha[chosen_global]
    gamma_chosen = gamma[chosen_global]
    folded = -(
        jnp.dot(gamma_rows, alpha_chosen.T, precision=highest)
        + jnp.dot(alpha_rows, gamma_chosen.T, precision=highest)
    )
    support_weights = (
        folded - equal_mask * (0.5 * folded + ridge_scale * intersection / SUPPORT)
    ) * keep_mask
    row_grad, row_map_grad, chosen_grad, chosen_map_grad = blocked_backward(
        row_images, row_maps, chosen_images, chosen_maps, support_weights, True
    )
    col_grad = place_blocks(chosen_grad, row_index, row_count, own_count, picks)
    col_map_grad = place_blocks(chosen_map_grad, row_index, row_count, own_count, picks)
    cross_grad, cross_map_grad, _, _ = blocked_backward(
        row_images, row_maps, target_images, target_maps, cross_weights, False
    )
    row_grad = row_grad + cross_grad
    row_map_grad = row_map_grad + cross_map_grad
    row_send = jnp.concatenate([row_grad, row_map_grad], axis=1)
    col_send = jnp.concatenate([col_grad, col_map_grad], axis=1)
    row_whole = lax.psum(row_send, "col")
    col_whole = lax.psum(col_send, "row")
    row_back = lax.dynamic_slice_in_dim(row_whole, col_index * own_count, own_count, 0)
    col_back = lax.dynamic_slice_in_dim(col_whole, row_index * own_count, own_count, 0)
    combined = row_back + col_back
    support_grad = combined[:, :channels] + self_back(own_support, combined[:, channels:])
    own_start = (row_index * col_count + col_index) * own_count
    label_grad = lax.dynamic_slice_in_dim(gamma, own_start, own_count, 0)
    return (support_grad, label_grad, 0.5 * loss_sum)


def solution(mesh):
    return jax.shard_map(
        body,
        mesh=mesh,
        in_specs=(
            P(("row", "col"), None, None, None),
            P(("row", "col")),
            P(("row", "col"), None, None, None),
            P(("row", "col")),
            P(("row", "col"), None),
            P(),
        ),
        out_specs=(P(("row", "col"), None, None), P(("row", "col"), None), P()),
        check_vma=False,
    )
```

profile of v0, /device:TPU:0, one launch (start us, length us, event | category | flops | bytes accessed | tf_op | source)
XLA Modules:
  0.0 1061.8 jit_solution(16985162748943276678)
XLA Ops:
  13.4 10.3 all_gather.19
  24.6 69.7 %all_gather.22 = f32[256,10]{1,0:T(8,128)S(1)} all-gather(f32[8,10]{1,0:T(8,128)S(1)} %copy-done.22), channel_id=1, replica_groups=mesh['row'=4,'col'=8] {'row','col'}, dimensions={0}, use_global_device_ids=true | all-gather | bytes 10560 | tf_op jit(solution)/shard_map/all_gather | solution.py:265
  94.9 7.8 all_gather.21
  107.6 80.1 %while.70 = (s32[]{:T(128)}, f32[6,64,4]{1,2,0:T(4,128)S(1)}, f32[64,3,1024]{2,0,1:T(8,128)S(1)}, f32[6,4,3,1024]{3,1,2,0:T(4,128)S(1)}, f32[64,3,1024]{2,0,1:T(...) while((s32[]{:T(128)}, f32[6,64,4]{1,2,0:T(4,128)S(1)}, f32[64,3,1024]{2,0,1:T(8,128)S(1)}, ...), condition=%wide.region_4.6_spmd, body=%wide.region_2.5_spmd.sunk | while | flops 19931136 | bytes 54733908 | solution.py:127
  117.9 3.1 multiply_reduce_fusion.27
  131.2 3.1 multiply_reduce_fusion.27
  144.4 3.1 multiply_reduce_fusion.27
  157.7 3.1 multiply_reduce_fusion.27
  170.9 3.1 multiply_reduce_fusion.27
  184.2 3.1 multiply_reduce_fusion.27
  187.8 65.5 %all-gather = f32[32,64,24]{1,2,0:T(8,128)S(1)} all-gather(f32[1,64,24]{1,2,0:T(8,128)S(1)} %select_bitcast_fusion.1), channel_id=1, replica_groups=mesh['row'=4,'col'=8] {'row','col'}, dimensions={0}, use_global_device_ids=true | all-gather | bytes 202752 | tf_op jit(solution)/shard_map/all_gather | solution.py:264
  258.8 11.7 %cholesky.49 = f32[128,128]{1,0:T(8,128)S(1)} custom-call(f32[128,128]{1,0:T(8,128)S(1)} %cholesky.115), custom_call_target="Cholesky" | custom-call | tf_op jit(solution)/shard_map/jit(cholesky)/cholesky | solution.py:269
  270.6 9.8 custom-call.17
  280.9 11.7 %cholesky.103 = f32[128,128]{1,0:T(8,128)S(1)} custom-call(f32[128,128]{1,0:T(8,128)S(1)} %convolution_subtract_fusion), custom_call_target="Cholesky" | custom-call | tf_op jit(solution)/shard_map/jit(cholesky)/cholesky | solution.py:269
  295.7 4.3 while.74
  300.6 20.5 %custom-call.29 = f32[2,128,128]{1,2,0:T(8,128)S(1)} custom-call(f32[2,128,128]{2,1,0:T(8,128)} %copy-done.27), custom_call_target="InvertDiagBlocksLowerTriangular" | custom-call | tf_op jit(solution)/shard_map/triangular_solve/custom-call.4 | solution.py:173
  323.0 117.2 %while.71 = (s32[]{:T(128)}, f32[8,64,4]{1,2,0:T(4,128)}, f32[64,3,1024]{2,0,1:T(8,128)S(1)}, f32[8,4,3,1024]{3,1,2,0:T(4,128)}, f32[64,3,1024]{2,0,1:T(8,128)S(1)}, /*index=5*/f32[8,4,3,1024]{3,1,2,0:T(4,128)}, s32[]{:T(128)}) while((s32[]{:T(128)}, f32[8,64,4]{1,2,0:T(4,128)}, f32[64,3,1024]{2,0,1:T(8,128)S(1)}, ...), condition=%wide.region_14.16_spmd, body=%wide.region_12.15_spmd.sunk | while | flops 19931136 | bytes 54733392 | solution.py:127
  392.6 3.1 multiply_reduce_fusion.28
  443.1 6.6 psum.35
  454.0 20.6 %all-reduce.111 = (f32[64,10]{0,1:T(8,128)S(1)}, f32[]{:T(128)}) all-reduce(f32[64,10]{0,1:T(8,128)} %fusion.91, f32[]{:T(128)} %multiply_reduce_fusion.19), channel_id=1, replica_groups=mesh['row'=4,'col'=8] {'col'}, use_global_device_ids=true, to_apply=%region_16.20 | all-reduce | flops 641 | bytes 5128 | tf_op jit(solution)/shard_map/psum | solution.py:275
  474.6 5.2 all-gather.1
  489.0 222.6 %while.72 = (s32[]{:T(128)}, f32[64,3,1024]{2,0,1:T(8,128)S(1)}, f32[64,3,1024]{2,0,1:T(8,128)S(1)}, f32[6,4,3,1024]{3,1,0,2:T(4,128)}, f32[6,4,3,1024]{3,1,0,2:...) while((s32[]{:T(128)}, f32[64,3,1024]{2,0,1:T(8,128)S(1)}, ...), condition=%wide.region_31.35_spmd.clone, body=%wide.region_18.34_spmd.clone.sunk | while | flops 38808064 | bytes 129204872 | solution.py:152
  719.3 243.5 %while.73 = (s32[]{:T(128)}, f32[64,3,1024]{2,0,1:T(8,128)S(1)}, f32[64,3,1024]{2,0,1:T(8,128)S(1)}, f32[64,3,1024]{2,0,1:T(8,128)S(1)}, f32[8,4,3,1024]{3,1,2,0...) while((s32[]{:T(128)}, f32[64,3,1024]{2,0,1:T(8,128)S(1)}, ...), condition=%wide.region_39.43_spmd.clone, body=%wide.region_32.42_spmd.clone.sunk | while | flops 36203008 | bytes 120111224 | solution.py:152
  967.8 83.4 %all-reduce.115.cloned.1.call-done = f32[64,6,1024]{2,0,1:T(8,128)} async-done(((f32[64,6,1024]{2,0,1:T(8,128)}), f32[64,6,1024]{2,0,1:T(8,128)}) %all-reduce.115.cloned.1.call-update) | async-done | bytes 1572880 | tf_op jit(solution)/shard_map/psum | solution.py:304
  (1050 shorter events, 657.0 us)
Async XLA Ops:
  7.2 3.4 copy-start.11
  7.2 99.0 %all-gather.4.cloned.1.call-start = ((), (), s32[]{:S(2)}) async-start(), calls=%async_computation | async-start | bytes 1769472 | tf_op jit(solution)/shard_map/all_gather | solution.py:223
  7.2 4.8 copy-start.17
  7.2 4.8 copy-start.19
  10.9 1.6 copy-start.9
  13.4 954.4 %all-reduce.117.cloned.1.call-start = ((), (), s32[]{:S(2)}) async-start(), calls=%async_computation.2 | async-start | bytes 1572864 | tf_op jit(solution)/shard_map/psum | solution.py:305
  102.8 1.8 copy-start.23
  105.5 82.2 %copy-start.24 = (s32[24]{0:T(128)}, s32[24]{0:T(128)S(1)}, u32[]{:S(2)}) copy-start(s32[24]{0:T(128)S(1)} %fusion.81) | copy-start | bytes 292
  105.5 82.2 %copy-start.25 = (pred[24]{0:T(512)(128)(4,1)}, pred[24]{0:T(512)(128)(4,1)S(1)}, u32[]{:S(2)}) copy-start(pred[24]{0:T(512)(128)(4,1)S(1)} %get-tuple-element.1339) | copy-start | bytes 76
  105.5 82.2 %copy-start.26 = (pred[24]{0:T(512)(128)(4,1)}, pred[24]{0:T(512)(128)(4,1)S(1)}, u32[]{:S(2)}) copy-start(pred[24]{0:T(512)(128)(4,1)S(1)} %get-tuple-element.1340) | copy-start | bytes 76
  187.7 66.6 %copy-start.7 = (f32[6,4,3,1024]{3,1,2,0:T(4,128)}, f32[6,4,3,1024]{3,1,2,0:T(4,128)S(1)}, u32[]{:S(2)}) copy-start(f32[6,4,3,1024]{3,1,2,0:T(4,128)S(1)} %get-tuple-element.2067) | copy-start | bytes 884740
  187.7 66.9 %copy-start.8 = (f32[6,4,3,1024]{3,1,2,0:T(4,128)}, f32[6,4,3,1024]{3,1,2,0:T(4,128)S(1)}, u32[]{:S(2)}) copy-start(f32[6,4,3,1024]{3,1,2,0:T(4,128)S(1)} %get-tuple-element.2068) | copy-start | bytes 884740
  323.0 126.7 %copy-start.16 = (f32[32,10]{0,1:T(8,128)S(1)}, f32[32,10]{0,1:T(8,128)}, u32[]{:S(2)}) copy-start(f32[32,10]{0,1:T(8,128)} %reshape.516) | copy-start | bytes 3844
  440.2 48.8 %copy-start.2 = (f32[64,3,1024]{2,0,1:T(8,128)S(1)}, f32[64,3,1024]{2,0,1:T(8,128)}, u32[]{:S(2)}) copy-start(f32[64,3,1024]{2,0,1:T(8,128)} %custom-call.22) | copy-start | bytes 2359300
  440.2 48.8 %copy-start.4 = (f32[64,3,1024]{2,0,1:T(8,128)S(1)}, f32[64,3,1024]{2,0,1:T(8,128)}, u32[]{:S(2)}) copy-start(f32[64,3,1024]{2,0,1:T(8,128)} %custom-call.23) | copy-start | bytes 2359300
  483.9 5.1 copy-start.12
  484.3 4.7 copy-start.14
  711.7 5.8 copy-start.3
  711.7 5.8 copy-start.5
  717.6 1.6 copy-start.1
  718.7 332.5 %all-reduce.115.cloned.1.call-start = ((), (), s32[]{:S(2)}) async-start(), calls=%async_computation.1 | async-start | bytes 3145728 | tf_op jit(solution)/shard_map/psum | solution.py:304
  965.6 86.7 %copy-start.18 = (pred[1024]{0:T(1024)(128)(4,1)S(1)}, pred[1024]{0:T(1024)(128)(4,1)}, u32[]{:S(2)}) copy-start(pred[1024]{0:T(1024)(128)(4,1)} %copy-done.17) | copy-start | bytes 3076
  965.6 86.7 %copy-start.20 = (pred[1024]{0:T(1024)(128)(4,1)S(1)}, pred[1024]{0:T(1024)(128)(4,1)}, u32[]{:S(2)}) copy-start(pred[1024]{0:T(1024)(128)(4,1)} %copy-done.19) | copy-start | bytes 3076
  965.6 87.6 %copy-start.10 = (f32[8,3,1024]{2,1,0:T(4,128)S(1)}, f32[8,3,1024]{2,1,0:T(4,128)}, u32[]{:S(2)}) copy-start(f32[8,3,1024]{2,1,0:T(4,128)} %copy-done.9) | copy-start | bytes 294916
  (7 other events, 5.9 us)
Sparse Core Ops, SparseCore 0:
  13.5 47.3 all-gather.3
  718.8 31.1 all-reduce.116
  965.7 85.3 all-reduce.114
where the time goes:
time: 1070 us; the launch traced here: 1060 us
  other arithmetic  564 us (53%)
  blocking collectives  186 us (17%)
  local copies, waits for them, and re-layouts  158 us (15%)
  waiting for transfers between devices  83.5 us (8%)
  loops' own time  41.1 us (4%)
  between operations  19.1 us (2%)
  matrix products  11 us (1%)
    div x56, other arithmetic, arc(): value = scale_map * (sine + (jnp.pi - angle) * cosine) / jnp.pi  165 us
    psum x1, waiting for transfers between devices, body(): row_whole = lax.psum(row_send, 'col')  83.4 us
    add x133, other arithmetic, average(): across = surface + leftward + rightward  83.2 us
    all_gather x1, blocking collectives, body(): lax.all_gather(support_labels, ('row', 'col'), axis=0, tiled=True)  69.7 us
    all_gather x1, blocking collectives, body(): lax.all_gather(support_tile, ('row', 'col'), axis=0, tiled=True)  65.5 us
    mul x40, other arithmetic, pair_backward(): grad = average(grad * slopes[layer])  56.8 us
    reduce_sum x24, other arithmetic, pair_backward(): first_parts.insert(0, jnp.sum(scaled, axis=1) / first_maps[:, layer])  53.7 us
    slice x135, local copies, waits for them, and re-layouts, shifted(): return jnp.concatenate([padding, surface[..., :extent + offset]], axis=-1)  49 us
  transfers between devices with their start and end apart: 3, of which 1 were waited for; matrix products, arithmetic and copies ran while one was open for 24% of the time, Pallas kernels for 0%

commit v1 on v0

--- a/solution.py
+++ b/solution.py
@@ -301,7 +301,7 @@
     row_map_grad = row_map_grad + cross_map_grad
     row_send = jnp.concatenate([row_grad, row_map_grad], axis=1)
     col_send = jnp.concatenate([col_grad, col_map_grad], axis=1)
-    row_whole = lax.psum(row_send, "col")
+    row_whole = jnp.sum(jax.lax.all_gather(row_send, "col"), axis=0)
     col_whole = lax.psum(col_send, "row")
     row_back = lax.dynamic_slice_in_dim(row_whole, col_index * own_count, own_count, 0)
     col_back = lax.dynamic_slice_in_dim(col_whole, row_index * own_count, own_count, 0)

time: 1070 us -> 1140 us (1.065)
  waiting for transfers between devices: 83.5 us -> 200 us
  other arithmetic: 564 us -> 525 us
  loops' own time: 41.1 us -> 23.7 us
  local copies, waits for them, and re-layouts: 158 us -> 173 us
    all_gather x0 -> x1, waiting for transfers between devices: none -> 169 us  [body(): row_whole = jnp.sum(jax.lax.all_gather(row_send, 'col'), axis=0)]
    psum x1 -> x0, waiting for transfers between devices: 83.4 us -> none  [body(): row_whole = lax.psum(row_send, 'col')]
    psum x1, waiting for transfers between devices: 0.02 us -> 30.6 us  [body(): col_whole = lax.psum(col_send, 'row')]
    another operation x2, loops' own time: 38.8 us -> 21.2 us  [blocked_backward(): lax.scan(one_block, start, (second.reshape((block_count, block_width) + s...]
    add x14, other arithmetic: 24.2 us -> 6.79 us  [one_block(): carry[0] + grad_first]
    while x0 -> x88, local copies, waits for them, and re-layouts: none -> 16.9 us
  transfers between devices with their start and end apart: 3 -> 3, of which waited for: 1 -> 2; matrix products, arithmetic and copies ran while one was open for 24% -> 1% of each run, Pallas kernels for 0% -> 0%
where the time goes in v1:
time: 1140 us; the launch traced here: 1130 us
  other arithmetic  525 us (46%)
  waiting for transfers between devices  200 us (18%)
  blocking collectives  184 us (16%)
  local copies, waits for them, and re-layouts  173 us (15%)
  loops' own time  23.7 us (2%)
  between operations  19.3 us (2%)
    all_gather x1, waiting for transfers between devices, body(): row_whole = jnp.sum(jax.lax.all_gather(row_send, 'col'), axis=0)  169 us
    div x56, other arithmetic, arc(): value = scale_map * (sine + (jnp.pi - angle) * cosine) / jnp.pi  165 us
    add x133, other arithmetic, average(): across = surface + leftward + rightward  83.4 us
    all_gather x1, blocking collectives, body(): lax.all_gather(support_labels, ('row', 'col'), axis=0, tiled=True)  71.3 us
    all_gather x1, blocking collectives, body(): lax.all_gather(support_tile, ('row', 'col'), axis=0, tiled=True)  65.6 us
    mul x40, other arithmetic, pair_backward(): grad = average(grad * slopes[layer])  57 us
    reduce_sum x24, other arithmetic, pair_backward(): first_parts.insert(0, jnp.sum(scaled, axis=1) / first_maps[:, layer])  53.7 us
    slice x135, local copies, waits for them, and re-layouts, shifted(): return jnp.concatenate([surface[..., offset:], padding], axis=-1)  49.1 us
  transfers between devices with their start and end apart: 3, of which 2 were waited for; matrix products, arithmetic and copies ran while one was open for 1% of the time, Pallas kernels for 0%

profile of v1, /device:TPU:0, one launch (start us, length us, event | category | flops | bytes accessed | tf_op | source)
XLA Modules:
  0.0 1131.6 jit_solution(16989059242025566253)
XLA Ops:
  15.9 71.3 %all_gather.28 = f32[256,10]{1,0:T(8,128)S(1)} all-gather(f32[8,10]{1,0:T(8,128)S(1)} %copy-done.30), channel_id=1, replica_groups=mesh['row'=4,'col'=8] {'row','col'}, dimensions={0}, use_global_device_ids=true | all-gather | bytes 10560 | tf_op jit(solution)/shard_map/all_gather | solution.py:265
  88.5 7.5 all_gather.27
  97.8 8.8 all_gather.25
  110.6 85.1 %while.70 = (s32[]{:T(128)}, f32[6,64,4]{1,2,0:T(4,128)S(1)}, f32[64,3,1024]{2,0,1:T(8,128)S(1)}, f32[6,4,3,1024]{3,1,2,0:T(4,128)S(1)}, f32[64,3,1024]{2,0,1:T(...) while((s32[]{:T(128)}, f32[6,64,4]{1,2,0:T(4,128)S(1)}, f32[64,3,1024]{2,0,1:T(8,128)S(1)}, ...), condition=%wide.region_4.6_spmd, body=%wide.region_2.5_spmd.sunk | while | flops 19931136 | bytes 54733916 | solution.py:127
  121.7 3.1 multiply_reduce_fusion.27
  135.8 3.1 multiply_reduce_fusion.27
  164.0 3.1 multiply_reduce_fusion.27
  178.0 3.1 multiply_reduce_fusion.27
  192.1 3.1 multiply_reduce_fusion.27
  195.8 65.6 %all-gather.1 = f32[32,64,24]{1,2,0:T(8,128)S(1)} all-gather(f32[1,64,24]{1,2,0:T(8,128)S(1)} %select_bitcast_fusion.1), channel_id=1, replica_groups=mesh['row'=4,'col'=8] {'row','col'}, dimensions={0}, use_global_device_ids=true | all-gather | bytes 202752 | tf_op jit(solution)/shard_map/all_gather | solution.py:264
  266.8 11.7 %cholesky.49 = f32[128,128]{1,0:T(8,128)S(1)} custom-call(f32[128,128]{1,0:T(8,128)S(1)} %cholesky.115), custom_call_target="Cholesky" | custom-call | tf_op jit(solution)/shard_map/jit(cholesky)/cholesky | solution.py:269
  279.8 9.8 custom-call.17
  290.8 11.7 %cholesky.103 = f32[128,128]{1,0:T(8,128)S(1)} custom-call(f32[128,128]{1,0:T(8,128)S(1)} %convolution_subtract_fusion), custom_call_target="Cholesky" | custom-call | tf_op jit(solution)/shard_map/jit(cholesky)/cholesky | solution.py:269
  303.3 112.7 %while.71 = (s32[]{:T(128)}, f32[8,64,4]{1,2,0:T(4,128)S(1)}, f32[64,3,1024]{2,0,1:T(8,128)S(1)}, f32[8,4,3,1024]{3,1,2,0:T(4,128)}, f32[64,3,1024]{2,0,1:T(8,12...) while((s32[]{:T(128)}, f32[8,64,4]{1,2,0:T(4,128)S(1)}, f32[64,3,1024]{2,0,1:T(8,128)S(1)}, ...), condition=%wide.region_14.16_spmd, body=%wide.region_12.15_spmd.sunk | while | flops 19931136 | bytes 54733916 | solution.py:127
  421.3 5.5 while.74
  426.9 20.5 %custom-call.29 = f32[2,128,128]{1,2,0:T(8,128)S(1)} custom-call(f32[2,128,128]{2,1,0:T(8,128)} %get-tuple-element.627), custom_call_target="InvertDiagBlocksLowerTriangular" | custom-call | tf_op jit(solution)/shard_map/triangular_solve/custom-call.4 | solution.py:173
  448.8 5.8 psum.28
  456.3 20.5 %all-reduce.111 = (f32[64,10]{0,1:T(8,128)S(1)}, f32[]{:T(128)}) all-reduce(f32[64,10]{0,1:T(8,128)S(1)} %fusion.88, f32[]{:T(128)} %multiply_reduce_fusion.19), channel_id=1, replica_groups=mesh['row'=4,'col'=8] {'col'}, use_global_device_ids=true, to_apply=%region_16.20 | all-reduce | flops 641 | bytes 5128 | tf_op jit(solution)/shard_map/psum | solution.py:275
  476.7 5.2 all-gather.2
  487.5 231.2 %while.73 = (s32[]{:T(128)}, f32[64,3,1024]{2,0,1:T(8,128)}, f32[64,3,1024]{2,0,1:T(8,128)}, f32[64,3,1024]{2,0,1:T(8,128)S(1)}, f32[8,4,3,1024]{3,1,2,0:T(4,128...) while((s32[]{:T(128)}, f32[64,3,1024]{2,0,1:T(8,128)}, ...), condition=%wide.region_39.43_spmd.clone, body=%wide.region_32.42_spmd.clone.sunk | while | flops 36203008 | bytes 132694256 | solution.py:152
  719.7 187.5 %while.72 = (s32[]{:T(128)}, f32[64,3,1024]{2,0,1:T(8,128)S(1)}, f32[64,3,1024]{2,0,1:T(8,128)S(1)}, f32[6,4,3,1024]{3,1,0,2:T(4,128)}, f32[6,4,3,1024]{3,1,0,2:...) while((s32[]{:T(128)}, f32[64,3,1024]{2,0,1:T(8,128)S(1)}, ...), condition=%wide.region_31.35_spmd.clone, body=%wide.region_18.34_spmd.clone.sunk | while | flops 38808064 | bytes 129253584 | solution.py:152
  914.7 169.1 %all-gather.8.cloned.1.call-done = f32[512,6,1024]{2,0,1:T(8,128)} async-done(((f32[64,6,1024]{2,0,1:T(8,128)}), f32[512,6,1024]{2,0,1:T(8,128)}) %all-gather.8.cloned.1.call-update) | async-done | bytes 12582928 | tf_op jit(solution)/shard_map/all_gather | solution.py:304
  1083.9 6.2 reduce_sum.391
  1090.1 30.6 %all-reduce.114.cloned.1.call-done = f32[32,6,1024]{2,1,0:T(8,128)} async-done(((f32[32,6,1024]{2,1,0:T(8,128)}), f32[32,6,1024]{2,1,0:T(8,128)}) %all-reduce.114.cloned.1.call-update) | async-done | bytes 786448 | tf_op jit(solution)/shard_map/psum | solution.py:305
  (1154 shorter events, 628.8 us)
Async XLA Ops:
  7.2 101.9 %all-gather.6.cloned.1.call-start = ((), (), s32[]{:S(2)}) async-start(), calls=%async_computation | async-start | bytes 1769472 | tf_op jit(solution)/shard_map/all_gather | solution.py:223
  7.2 5.9 copy-start.21
  7.2 5.9 copy-start.23
  14.3 1069.5 %all-gather.8.cloned.1.call-start = ((), (), s32[]{:S(2)}) async-start(), calls=%async_computation.2 | async-start | bytes 14155776 | tf_op jit(solution)/shard_map/all_gather | solution.py:304
  108.4 87.3 %copy-start.33 = (s32[24]{0:T(128)}, s32[24]{0:T(128)S(1)}, u32[]{:S(2)}) copy-start(s32[24]{0:T(128)S(1)} %fusion.78) | copy-start | bytes 292
  108.4 87.3 %copy-start.35 = (pred[24]{0:T(512)(128)(4,1)}, pred[24]{0:T(512)(128)(4,1)S(1)}, u32[]{:S(2)}) copy-start(pred[24]{0:T(512)(128)(4,1)S(1)} %get-tuple-element.1293) | copy-start | bytes 76
  108.4 87.3 %copy-start.37 = (pred[24]{0:T(512)(128)(4,1)}, pred[24]{0:T(512)(128)(4,1)S(1)}, u32[]{:S(2)}) copy-start(pred[24]{0:T(512)(128)(4,1)S(1)} %get-tuple-element.1294) | copy-start | bytes 76
  195.7 67.1 %copy-start.7 = (f32[6,4,3,1024]{3,1,2,0:T(4,128)}, f32[6,4,3,1024]{3,1,2,0:T(4,128)S(1)}, u32[]{:S(2)}) copy-start(f32[6,4,3,1024]{3,1,2,0:T(4,128)S(1)} %get-tuple-element.2022) | copy-start | bytes 884740
  266.5 36.7 %copy-start.10 = (f32[8,4,3,1024]{3,1,2,0:T(4,128)S(1)}, f32[8,4,3,1024]{3,1,2,0:T(4,128)}, u32[]{:S(2)}) copy-start(f32[8,4,3,1024]{3,1,2,0:T(4,128)} %copy.279) | copy-start | bytes 1179652
  303.3 112.8 %copy-start.32 = (f32[128]{0:T(128)S(1)}, f32[128]{0:T(128)}, u32[]{:S(2)}) copy-start(f32[128]{0:T(128)} %get-tuple-element.1246) | copy-start | bytes 1540
  303.3 118.0 %copy-start.38 = (s32[2]{0:T(128)S(1)}, s32[2]{0:T(128)}, u32[]{:S(2)}) copy-start(s32[2]{0:T(128)} %iota_multiply_fusion) | copy-start | bytes 28
  418.6 28.8 %copy-start.13 = (f32[256,10]{1,0:T(8,128)S(1)}, f32[256,10]{1,0:T(8,128)}, u32[]{:S(2)}) copy-start(f32[256,10]{1,0:T(8,128)} %copy-done.12) | copy-start | bytes 30724
  419.5 28.1 %copy-start.27 = (f32[128,10]{0,1:T(8,128)S(1)}, f32[128,10]{0,1:T(8,128)}, u32[]{:S(2)}) copy-start(f32[128,10]{0,1:T(8,128)} %copy.308) | copy-start | bytes 15364
  421.2 33.4 %copy-start.20 = (f32[32,10]{0,1:T(8,128)S(1)}, f32[32,10]{0,1:T(8,128)}, u32[]{:S(2)}) copy-start(f32[32,10]{0,1:T(8,128)} %reshape.516) | copy-start | bytes 3844
  448.7 28.0 %copy-start.25 = (f32[64,10]{0,1:T(8,128)}, f32[64,10]{0,1:T(8,128)S(1)}, u32[]{:S(2)}) copy-start(f32[64,10]{0,1:T(8,128)S(1)} %fusion.59) | copy-start | bytes 7684
  487.5 231.3 %copy-start.26 = (f32[64,10]{0,1:T(8,128)S(1)}, f32[64,10]{0,1:T(8,128)}, u32[]{:S(2)}) copy-start(f32[64,10]{0,1:T(8,128)} %copy-done.25) | copy-start | bytes 7684
  487.5 231.3 %copy-start.34 = (s32[24]{0:T(128)S(1)}, s32[24]{0:T(128)}, u32[]{:S(2)}) copy-start(s32[24]{0:T(128)} %copy-done.33) | copy-start | bytes 292
  487.5 231.3 %copy-start.36 = (pred[24]{0:T(512)(128)(4,1)S(1)}, pred[24]{0:T(512)(128)(4,1)}, u32[]{:S(2)}) copy-start(pred[24]{0:T(512)(128)(4,1)} %copy-done.35) | copy-start | bytes 76
  487.5 232.2 %copy-start = (f32[64,3,1024]{2,0,1:T(8,128)S(1)}, f32[64,3,1024]{2,0,1:T(8,128)}, u32[]{:S(2)}) copy-start(f32[64,3,1024]{2,0,1:T(8,128)} %custom-call.23) | copy-start | bytes 2359300
  487.5 232.2 %copy-start.1 = (f32[64,3,1024]{2,0,1:T(8,128)S(1)}, f32[64,3,1024]{2,0,1:T(8,128)}, u32[]{:S(2)}) copy-start(f32[64,3,1024]{2,0,1:T(8,128)} %custom-call.22) | copy-start | bytes 2359300
  910.0 210.7 %all-reduce.114.cloned.1.call-start = ((), (), s32[]{:S(2)}) async-start(), calls=%async_computation.1 | async-start | bytes 2097152 | tf_op jit(solution)/shard_map/psum | solution.py:305
  1083.9 38.1 %copy-start.22 = (pred[1024]{0:T(1024)(128)(4,1)S(1)}, pred[1024]{0:T(1024)(128)(4,1)}, u32[]{:S(2)}) copy-start(pred[1024]{0:T(1024)(128)(4,1)} %copy-done.21) | copy-start | bytes 3076
  1083.9 38.1 %copy-start.24 = (pred[1024]{0:T(1024)(128)(4,1)S(1)}, pred[1024]{0:T(1024)(128)(4,1)}, u32[]{:S(2)}) copy-start(pred[1024]{0:T(1024)(128)(4,1)} %copy-done.23) | copy-start | bytes 3076
  1090.1 32.8 %copy-start.9 = (f32[8,3,1024]{2,1,0:T(4,128)S(1)}, f32[8,3,1024]{2,1,0:T(4,128)}, u32[]{:S(2)}) copy-start(f32[8,3,1024]{2,1,0:T(4,128)} %copy-done.8) | copy-start | bytes 294916
  (56 other events, 79.6 us)
Sparse Core Ops, SparseCore 0:
  14.5 47.3 all-gather.5
  910.2 173.6 all-gather.7
  1086.2 34.4 all-reduce.113
